TPU v7x, 512 devices: a whole 4x8x8 slice. The times are simulated.
512 devices in a mesh: leaf: 32 (over x, y), front: 16 (over z, core).
Axes of the slice: x: 4, y: 8, z: 8, core: 2. Of those that a mesh axis runs over, the one named last changes fastest.
Arguments:
- child_pivot: float32 [32, 512, 512], P('leaf', 'front')
- child_panel: float32 [32, 2048, 512], P('leaf', 'front'), may hold values from -0.9 to 0.9
- anc_front: float32 [32, 16, 512, 512], P('leaf', 'front')
- dest_list: int32 [32, 16], replicated, may hold values from 0 to 31, as said below
- col_list: int32 [32, 16], replicated, may hold values from 0 to 3, as said below
- row_list: int32 [32, 16], replicated, may hold values from 0 to 3, as said below
Outputs:
- child_lower: float32 [32, 512, 512], P('leaf', 'front')
- child_factor: float32 [32, 2048, 512], P('leaf', 'front')
- anc_factor: float32 [32, 16, 512, 512], P('leaf', 'front')
Inputs may be any that keep to these rules, and one draw needn't show every extreme that they name: dest_list[g, j] is g with exactly one bit of its index flipped; every group that row g names is named there by exactly 4 column blocks, so row g names 4 different groups. `col_list`: column blocks of one group that name the same group in dest_list have different entries here. row_list[g, f] is 1 or more for f < 4.
All inputs are finite; a program needn't handle non-finite values.
Results may differ from a plain program's by a relative error of at most 0.0001.
Values sent between devices are 32-bit elements; how exact they have to be, the bound alone decides.
No kernel may reach another device: no remote copies, remote signals or barrier semaphores. Data moves between devices by JAX's collectives and lax.ppermute only.
A program may use at most 64 MiB of HBM per device.

v0:
```python
import jax
import jax.numpy as jnp
from jax import lax
from jax.experimental import pallas as pl
from jax.experimental.pallas import tpu as pltpu
from jax.sharding import PartitionSpec as P

F32 = jnp.float32
BLK = 128
SUB = 8


def dot(a, b, ca=1, cb=0):
    return lax.dot_general(
        a,
        b,
        (((ca,), (cb,)), ((), ())),
        precision=lax.Precision.HIGHEST,
        preferred_element_type=F32,
    )


def split3(x):
    high = x.astype(jnp.bfloat16).astype(F32)
    rest = x - high
    mid = rest.astype(jnp.bfloat16).astype(F32)
    return high, mid, rest - mid


def eliminate(m_ref, k, here):
    base = SUB * k
    last = base + SUB >= BLK
    ra = [jnp.broadcast_to(here[0][i : i + 1], (SUB, BLK)) for i in range(SUB)]
    rb = [jnp.broadcast_to(here[1][i : i + 1], (SUB, BLK)) for i in range(SUB)]
    d = {}
    for i in range(SUB):
        for j in range(i, SUB):
            d[i, j] = jnp.broadcast_to(ra[i][:, base + j : base + j + 1], (SUB, BLK))
    if not last:
        na = m_ref[base + SUB : base + 2 * SUB, :BLK]
        nb = m_ref[base + SUB : base + 2 * SUB, BLK:]
        c = [jnp.broadcast_to(na[:, base + q : base + q + 1], (SUB, BLK)) for q in range(SUB)]
    sub = lax.broadcasted_iota(jnp.int32, (SUB, BLK), 0)
    ua_all = ub_all = None
    for q in range(SUB):
        s = lax.rsqrt(d[q, q])
        low = {i: d[q, i] * s for i in range(q + 1, SUB)}
        for i in range(q + 1, SUB):
            for j in range(i, SUB):
                d[i, j] = d[i, j] - low[i] * low[j]
        ua = ra[q] * s
        ub = rb[q] * s
        for i in range(q + 1, SUB):
            ra[i] = ra[i] - low[i] * ua
            rb[i] = rb[i] - low[i] * ub
        if not last:
            cq = c[q] * s
            for j in range(q + 1, SUB):
                c[j] = c[j] - cq * low[j]
            na = na - cq * ua
            nb = nb - cq * ub
        ua_all = ua if q == 0 else jnp.where(sub == q, ua, ua_all)
        ub_all = ub if q == 0 else jnp.where(sub == q, ub, ub_all)
    u = jnp.concatenate([ua_all, ub_all], 1)
    m_ref[base : base + SUB, :] = u
    if last:
        return None
    if base + 2 * SUB < BLK:
        hi, mi, lo = split3(u)
        ah, am, al = hi[:, :BLK], mi[:, :BLK], lo[:, :BLK]
        left = jnp.concatenate([ah, ah, am, ah, al, am], 0).astype(jnp.bfloat16)
        right = jnp.concatenate([hi, mi, hi, lo, hi, mi], 0).astype(jnp.bfloat16)
        upd = lax.dot_general(
            left, right, (((0,), (0,)), ((), ())), preferred_element_type=F32
        )
        m_ref[base + 2 * SUB :, :] = m_ref[base + 2 * SUB :, :] - upd[base + 2 * SUB :, :]
    return na, nb


def factor(t, l_ref, x_ref, m_ref):
    n = t.shape[0]
    ri = lax.broadcasted_iota(jnp.int32, (BLK, BLK), 0)
    ci = lax.broadcasted_iota(jnp.int32, (BLK, BLK), 1)
    for r1 in range(BLK, n, BLK):
        zero = jnp.zeros((BLK, n - r1), F32)
        l_ref[r1 - BLK : r1, r1:] = zero
        x_ref[r1 - BLK : r1, r1:] = zero

    def rest(b):
        r0, r1 = b * BLK, (b + 1) * BLK
        inv = m_ref[:, BLK:]
        if r1 < n:
            u = dot(inv, t[r0:r1, r1:])
            for i in range(r1, n, BLK):
                side = u[:, i - r1 : i - r1 + BLK]
                t[i : i + BLK, i:] = t[i : i + BLK, i:] - dot(side, u[:, i - r1 :], 0, 0)
            l_ref[r1:, r0:r1] = u.T
        l_ref[r0:r1, r0:r1] = jnp.where(ci >= ri, m_ref[:, :BLK], 0.0).T
        x_ref[r0:r1, r0:r1] = inv
        if r0:
            x_ref[r0:r1, :r0] = -dot(inv, dot(l_ref[r0:r1, :r0], x_ref[:r0, :r0]))

    def step(b, carry):
        r0 = pl.multiple_of(b * BLK, BLK)
        m_ref[:, :BLK] = t[pl.ds(r0, BLK), pl.ds(r0, BLK)]
        m_ref[:, BLK:] = (ri == ci).astype(F32)
        here = (m_ref[:SUB, :BLK], m_ref[:SUB, BLK:])
        for k in range(BLK // SUB):
            here = eliminate(m_ref, k, here)
        for fixed in range(n // BLK):
            pl.when(b == fixed)(lambda fixed=fixed: rest(fixed))
        return carry

    lax.fori_loop(0, n // BLK, step, 0)


def child_kernel(info, own, other, panel, rows_out, f_out, w_out, t, l_ref, x_ref, m_ref):
    front = info[1]
    z, core = front // 2, front % 2
    slab = rows_out.shape[0]
    for q in range(own.shape[0] // slab):
        at = 2 * slab * (z ^ q)
        mine = pl.multiple_of(at + slab * core, slab)
        theirs = pl.multiple_of(at + slab * (1 - core), slab)
        t[pl.ds(mine, slab), :] = own[slab * q : slab * (q + 1), :]
        t[pl.ds(theirs, slab), :] = other[slab * q : slab * (q + 1), :]
    factor(t, l_ref, x_ref, m_ref)
    rows_out[...] = l_ref[pl.ds(pl.multiple_of(front * slab, slab), slab), :]
    half = x_ref.shape[0] // 2
    first = dot(panel[:, :half], x_ref[:half, :half], 1, 1)
    second = dot(panel[...], x_ref[half:, :], 1, 1)
    f_out[:, :half] = first
    f_out[:, half:] = second
    w_out[:, :half] = dot(f_out[...], x_ref[:, :half])
    w_out[:, half:] = dot(second, x_ref[half:, half:])


def anc_kernel(info, mine, near, across0, across1, rows_out, inv_out, t, l_ref, x_ref, m_ref):
    own = jnp.minimum(info[1], t.shape[0] // BLK - 1)
    for part, mask in ((mine, 0), (near, 2), (across0, 1), (across1, 3)):
        t[pl.ds(pl.multiple_of((own ^ mask) * BLK, BLK), BLK), :] = part[...]
    factor(t, l_ref, x_ref, m_ref)
    at = pl.multiple_of(own * BLK, BLK)
    rows_out[...] = l_ref[pl.ds(at, BLK), :]
    inv_out[...] = x_ref[pl.ds(at, BLK), :]


def update_kernel(info, w, panels, m0, m1, m2, m3, m4, u_ref, table):
    outs = (m0, m1, m2, m3, m4)
    wide = m0.shape[1] // BLK
    fronts = panels.shape[0]
    for i in range(len(outs) * wide):
        table[i] = -1
    for j in range(fronts):
        diff = info[2 + j] ^ info[0]
        level = sum((diff >= 2**b).astype(jnp.int32) for b in range(1, len(outs)))
        table[level * wide + info[2 + fronts + j]] = j
    for j in range(fronts):
        u_ref[j] = dot(w[...], panels[j], 1, 1)
    for level, out in enumerate(outs):
        for c in range(wide):
            j = table[level * wide + c]
            out[:, BLK * c : BLK * (c + 1)] = jnp.where(j >= 0, u_ref[jnp.maximum(j, 0)], 0.0)


def final_kernel(info, front_ref, r0, r1, r2, r3, r4, x_ref, lower, out, t):
    t[...] = front_ref[...]
    for level, got in enumerate((r0, r1, r2, r3, r4)):
        at = pl.multiple_of(info[34 + level] * BLK, BLK)
        t[pl.ds(at, BLK), :] = t[pl.ds(at, BLK), :] - got[...]
    n = t.shape[1]
    half = n // 2
    x = x_ref[...].reshape(n, n)
    out[:, :half] = dot(t[:, :half], x[:half, :half], 1, 1)
    out[:, half:] = dot(t[...], x[half:, :], 1, 1)

    @pl.when(info[1] < t.shape[1] // BLK)
    def _():
        out[:BLK, :] = lower[...]


VMEM = pl.BlockSpec(memory_space=pltpu.VMEM)
SMEM = pl.BlockSpec(memory_space=pltpu.SMEM)


def shape(*dims):
    return jax.ShapeDtypeStruct(dims, F32)


def make_info(group, front, levels, dest_list, col_list, row_list):
    leaves, fronts = dest_list.shape
    width = 2 + 2 * fronts + levels
    lane = jnp.arange(width)
    leaf = jnp.arange(leaves)[:, None]
    wide = jnp.concatenate(
        [
            jnp.zeros((leaves, 2), jnp.int32),
            dest_list,
            col_list,
            jnp.broadcast_to(row_at(row_list, front), (leaves, levels)),
        ],
        1,
    )
    level = lane - (2 + 2 * fronts)
    source = jnp.where(level >= 0, group ^ (1 << jnp.maximum(level, 0)), group)
    picked = jnp.sum(jnp.where(leaf == source[None, :], wide, 0), axis=0)
    return jnp.where(lane == 0, group, jnp.where(lane == 1, front, picked)).astype(jnp.int32)


def row_at(row_list, front):
    lane = jnp.arange(row_list.shape[1])
    return jnp.sum(jnp.where(lane == front, row_list, 0), axis=1, keepdims=True)


def per_device(child_pivot, child_panel, anc_front, dest_list, col_list, row_list):
    fronts = lax.axis_size("front")
    group, front = lax.axis_index("leaf"), lax.axis_index("front")
    slab = child_pivot.shape[1]
    n = child_panel.shape[2]
    levels = lax.axis_size("leaf").bit_length() - 1

    info = make_info(group, front, levels, dest_list, col_list, row_list)

    def pair_up(value, partner):
        pairs = [(2 * z + c, 2 * partner(z) + c) for z in range(fronts // 2) for c in range(2)]
        return lax.ppermute(value, "front", pairs)

    gathered = lax.all_gather(child_panel[0], "front", axis=0, tiled=False)

    mine = child_pivot[0]
    pair = jnp.concatenate([mine, pair_up(mine, lambda z: z ^ 1)], 0)
    top = anc_front[0, 0, :BLK]
    near = lax.ppermute(top, "front", [(f, f ^ 2) for f in range(n // BLK)])
    pair, info = lax.optimization_barrier((pair, info))
    parts = [pair]
    for k in (2, 4, 6):
        parts.append(pair_up(pair, lambda z, k=k: z ^ k))
    across = lax.ppermute(
        jnp.concatenate([top, near], 0), "front", [(f, f ^ 1) for f in range(n // BLK)]
    )
    square = pltpu.VMEM((n, n), F32)
    work = pltpu.VMEM((BLK, 2 * BLK), F32)
    anc_rows, anc_inv = pl.pallas_call(
        anc_kernel,
        grid=(1,),
        out_shape=(shape(BLK, n),) * 2,
        in_specs=[SMEM, VMEM, VMEM]
        + [pl.BlockSpec((BLK, n), lambda i, half=half: (half, 0)) for half in range(2)],
        out_specs=(VMEM, VMEM),
        scratch_shapes=[square, square, square, work],
        name="ancestor_cholesky",
    )(info, top, near, across, across)
    inverses = lax.all_gather(anc_inv, "front", axis=0, tiled=False)

    own = jnp.concatenate(parts, 0)
    other = lax.ppermute(own, "front", [(f, f ^ 1) for f in range(fronts)])
    lower_rows, panel, w = pl.pallas_call(
        child_kernel,
        out_shape=(shape(slab, n), shape(BLK, n), shape(BLK, n)),
        in_specs=[SMEM, VMEM, VMEM, VMEM],
        out_specs=(VMEM,) * 3,
        scratch_shapes=[square, square, square, work],
        name="child_cholesky",
    )(info, own, other, child_panel[0])

    messages = pl.pallas_call(
        update_kernel,
        out_shape=(shape(BLK, n),) * levels,
        in_specs=[SMEM, VMEM, VMEM],
        out_specs=(VMEM,) * levels,
        scratch_shapes=[
            pltpu.VMEM((fronts, BLK, BLK), F32),
            pltpu.SMEM((levels * (n // BLK),), jnp.int32),
        ],
        name="update",
    )(info, w, gathered)

    arrived = [None] * levels
    for level in (2, 4, 1, 3, 0):
        pairs = [(s, s ^ 2**level) for s in range(lax.axis_size("leaf"))]
        arrived[level] = lax.ppermute(messages[level], "leaf", pairs)

    anc_out = pl.pallas_call(
        final_kernel,
        out_shape=shape(n, n),
        grid=(1,),
        in_specs=[SMEM]
        + [VMEM] * (levels + 1)
        + [pl.BlockSpec((n // BLK, BLK, n), lambda i: (0, 0, 0)), VMEM],
        out_specs=VMEM,
        scratch_shapes=[square],
        name="finish",
    )(info, anc_front[0, 0], *arrived, inverses, anc_rows)
    return (lower_rows[None], panel[None], anc_out[None, None])


def solution(mesh):
    in_specs = (
        P("leaf", "front", None),
        P("leaf", "front", None),
        P("leaf", "front", None, None),
        P(),
        P(),
        P(),
    )
    out_specs = (P("leaf", "front", None), P("leaf", "front", None), P("leaf", "front", None, None))

    return jax.shard_map(
        per_device, mesh=mesh, in_specs=in_specs, out_specs=out_specs, check_vma=False
    )
```

profile of v0, /device:TPU:1, one launch (start us, length us, event | category | flops | bytes accessed | tf_op | source)
XLA Modules:
  0.0 147.0 jit_solution(17885647959152687022)
XLA Ops:
  7.9 1.0 slice_bitcast_fusion.mine
  8.9 4.8 %collective-permute-start.10 = (f32[128,512]{1,0:T(8,128)S(1)}, f32[128,512]{1,0:T(8,128)S(1)}, u32[]{:S(2)}, u32[]{:S(2)}) collective-permute-start(f32[128,512]{1,0:T(8,128)S(1)} %slice_bitcast_fusion.mine), channel_id=1, source_target_pairs={{0,2},{1,3},{2,0},{3,1},{16,18},{17,19},{18,16},{19,17},{32,34},{3... | collective-permute-start | bytes 786440 | tf_op jit(solution)/shard_map/ppermute | solution.py:233
  13.8 1.9 %collective-permute-start = (f32[32,512]{1,0:T(8,128)}, f32[32,512]{1,0:T(8,128)S(1)}, u32[]{:S(2)}, u32[]{:S(2)}) collective-permute-start(f32[32,512]{1,0:T(8,128)} %bitcast.13), channel_id=1, source_target_pairs={{0,2},{1,3},{2,0},{3,1},{4,6},{5,7},{6,4},{7,5},{8,10},{9,11},{10,... | collective-permute-start | bytes 196616 | tf_op jit(solution)/shard_map/ppermute | solution.py:226
  16.5 1.0 collective-permute-done.10.near
  17.5 8.4 %collective-permute-start.11 = (f32[256,512]{1,0:T(8,128)S(1)}, f32[256,512]{1,0:T(8,128)S(1)}, u32[]{:S(2)}, u32[]{:S(2)}) collective-permute-start(f32[256,512]{1,0:T(8,128)S(1)} %pad_maximum_fusion), channel_id=1, source_target_pairs={{0,1},{1,0},{2,3},{3,2},{16,17},{17,16},{18,19},{19,18},{32,33},{3... | collective-permute-start | bytes 1572872 | tf_op jit(solution)/shard_map/ppermute | solution.py:238
  26.0 0.9 fusion
  29.1 21.4 %ancestor_cholesky.1 = (f32[128,512]{1,0:T(8,128)}, f32[128,512]{1,0:T(8,128)}) custom-call(s32[39]{0:T(128)} %compare_select_fusion.2.info, f32[128,512]{1,0:T(8,128)} %copy-done, f32[128,512]{1,0:T(8,128)} %copy-done.2, f32[256,512]{1,0:T(8,128)} %copy-done.1, f32[256,512]{1,0:T(8,128)} %copy-done.1), custom_call_target="tpu_custom_call" | custom-call | tf_op jit(solution)/shard_map/ancestor_cholesky/pallas_call | solution.py:243
  50.5 1.9 %collective-permute-start.1 = (f32[64,512]{1,0:T(8,128)S(1)}, f32[64,512]{1,0:T(8,128)S(1)}, u32[]{:S(2)}, u32[]{:S(2)}) collective-permute-start(f32[64,512]{1,0:T(8,128)S(1)} %pad_maximum_fusion.1), channel_id=1, source_target_pairs={{0,4},{1,5},{2,6},{3,7},{4,0},{5,1},{6,2},{7,3},{8,12},{9,13},{10,... | collective-permute-start | bytes 393224 | tf_op jit(solution)/shard_map/ppermute | solution.py:226
  52.4 1.9 %collective-permute-start.2 = (f32[64,512]{1,0:T(8,128)S(1)}, f32[64,512]{1,0:T(8,128)S(1)}, u32[]{:S(2)}, u32[]{:S(2)}) collective-permute-start(f32[64,512]{1,0:T(8,128)S(1)} %pad_maximum_fusion.1), channel_id=1, source_target_pairs={{0,8},{1,9},{2,10},{3,11},{4,12},{5,13},{6,14},{7,15},{8,0},{9,1},... | collective-permute-start | bytes 393224 | tf_op jit(solution)/shard_map/ppermute | solution.py:226
  54.4 7.5 %collective-permute-start.3 = (f32[64,512]{1,0:T(8,128)S(1)}, f32[64,512]{1,0:T(8,128)S(1)}, u32[]{:S(2)}, u32[]{:S(2)}) collective-permute-start(f32[64,512]{1,0:T(8,128)S(1)} %pad_maximum_fusion.1), channel_id=1, source_target_pairs={{0,12},{1,13},{2,14},{3,15},{4,8},{5,9},{6,10},{7,11},{8,4},{9,5},... | collective-permute-start | bytes 393224 | tf_op jit(solution)/shard_map/ppermute | solution.py:226
  61.9 6.2 %collective-permute-done.1 = f32[64,512]{1,0:T(8,128)S(1)} collective-permute-done((f32[64,512]{1,0:T(8,128)S(1)}, f32[64,512]{1,0:T(8,128)S(1)}, u32[]{:S(2)}, u32[]{:S(2)}) %collective-permute-start.1) | collective-permute-done | bytes 131104 | tf_op jit(solution)/shard_map/ppermute | solution.py:226
  68.1 2.0 %collective-permute-done.3 = f32[64,512]{1,0:T(8,128)S(1)} collective-permute-done((f32[64,512]{1,0:T(8,128)S(1)}, f32[64,512]{1,0:T(8,128)S(1)}, u32[]{:S(2)}, u32[]{:S(2)}) %collective-permute-start.3) | collective-permute-done | bytes 131104 | tf_op jit(solution)/shard_map/ppermute | solution.py:226
  70.2 3.0 %collective-permute-start.4 = (f32[256,512]{1,0:T(8,128)S(1)}, f32[256,512]{1,0:T(8,128)S(1)}, u32[]{:S(2)}, u32[]{:S(2)}) collective-permute-start(f32[256,512]{1,0:T(8,128)S(1)} %constant_dynamic-update-slice_fusion.own), channel_id=1, source_target_pairs={{0,1},{1,0},{2,3},{3,2},{4,5},{5,4},{6,7},{7,6},{8,9},{9,8},{10,11... | collective-permute-start | bytes 1572872 | tf_op jit(solution)/shard_map/ppermute | solution.py:256
  73.2 1.3 collective-permute-done.4.other
  74.5 0.9 copy-done.4
  75.4 22.8 %child_cholesky.1 = (f32[32,512]{1,0:T(8,128)}, f32[128,512]{1,0:T(8,128)}, f32[128,512]{1,0:T(8,128)}) custom-call(s32[39]{0:T(128)} %compare_select_fusion.2.info, f32[256,512]{1,0:T(8,128)} %copy-done.3, f32[256,512]{1,0:T(8,128)} %copy-done.4, f32[128,512]{1,0:T(8,128)} %bitcast.12), custom_call_target="tpu_custom_call" | custom-call | tf_op jit(solution)/shard_map/child_cholesky/pallas_call | solution.py:257
  98.2 6.9 %update.1 = (f32[128,512]{1,0:T(8,128)}, f32[128,512]{1,0:T(8,128)}, f32[128,512]{1,0:T(8,128)}, f32[128,512]{1,0:T(8,128)}, f32[128,512]{1,0:T(8,128)}) custom-call(s32[39]{0:T(128)} %compare_select_fusion.2.info, f32[128,512]{1,0:T(8,128)} %get-tuple-element.19.w, f32[16,128,512]{2,1,0:T(8,128)} %all-gather.4.cloned.1.call-done.panels), custom_call_target="tpu_custom_call" | custom-call | tf_op jit(solution)/shard_map/update/pallas_call | solution.py:266
  105.1 1.9 %collective-permute-start.5 = (f32[128,512]{1,0:T(8,128)}, f32[128,512]{1,0:T(8,128)S(1)}, u32[]{:S(2)}, u32[]{:S(2)}) collective-permute-start(f32[128,512]{1,0:T(8,128)} %get-tuple-element.20), channel_id=1, source_target_pairs={{0,16},{16,0},{32,48},{48,32},{64,80},{80,64},{96,112},{112,96},{1... | collective-permute-start | bytes 786440 | tf_op jit(solution)/shard_map/ppermute | solution.py:281
  107.0 4.1 %collective-permute-start.6 = (f32[128,512]{1,0:T(8,128)}, f32[128,512]{1,0:T(8,128)S(1)}, u32[]{:S(2)}, u32[]{:S(2)}) collective-permute-start(f32[128,512]{1,0:T(8,128)} %get-tuple-element.21), channel_id=1, source_target_pairs={{0,32},{16,48},{32,0},{48,16},{64,96},{80,112},{96,64},{112,80},{1... | collective-permute-start | bytes 786440 | tf_op jit(solution)/shard_map/ppermute | solution.py:281
  111.1 4.7 %collective-permute-start.7 = (f32[128,512]{1,0:T(8,128)}, f32[128,512]{1,0:T(8,128)S(1)}, u32[]{:S(2)}, u32[]{:S(2)}) collective-permute-start(f32[128,512]{1,0:T(8,128)} %get-tuple-element.22), channel_id=1, source_target_pairs={{0,64},{16,80},{32,96},{48,112},{64,0},{80,16},{96,32},{112,48},{1... | collective-permute-start | bytes 786440 | tf_op jit(solution)/shard_map/ppermute | solution.py:281
  115.9 3.0 %collective-permute-start.8 = (f32[128,512]{1,0:T(8,128)}, f32[128,512]{1,0:T(8,128)S(1)}, u32[]{:S(2)}, u32[]{:S(2)}) collective-permute-start(f32[128,512]{1,0:T(8,128)} %get-tuple-element.23), channel_id=1, source_target_pairs={{0,128},{16,144},{32,160},{48,176},{64,192},{80,208},{96,224},{112... | collective-permute-start | bytes 786440 | tf_op jit(solution)/shard_map/ppermute | solution.py:281
  118.8 4.2 %collective-permute-start.9 = (f32[128,512]{1,0:T(8,128)}, f32[128,512]{1,0:T(8,128)S(1)}, u32[]{:S(2)}, u32[]{:S(2)}) collective-permute-start(f32[128,512]{1,0:T(8,128)} %get-tuple-element.24), channel_id=1, source_target_pairs={{0,256},{16,272},{32,288},{48,304},{64,320},{80,336},{96,352},{112... | collective-permute-start | bytes 786440 | tf_op jit(solution)/shard_map/ppermute | solution.py:281
  123.1 11.3 %collective-permute-done.6.r1 = f32[128,512]{1,0:T(8,128)S(1)} collective-permute-done((f32[128,512]{1,0:T(8,128)}, f32[128,512]{1,0:T(8,128)S(1)}, u32[]{:S(2)}, u32[]{:S(2)}) %collective-permute-start.6) | collective-permute-done | bytes 262176 | tf_op jit(solution)/shard_map/ppermute | solution.py:281
  135.6 4.6 %finish.1 = f32[512,512]{1,0:T(8,128)} custom-call(s32[39]{0:T(128)} %compare_select_fusion.2.info, f32[512,512]{1,0:T(8,128)} %bitcast.10, f32[128,512]{1,0:T(8,128)} %copy-done.5, f32[128,512]{1,0:T(8,128)} %copy-done.6, f32[128,512]{1,0:T(8,128)} %copy-done.7, f32[128,512]{1,0:T(8,128)} %copy-done.8, f32[128,512]{1,0:T(8,128)} %copy-done.9, ...), custom_call_target="tpu_custom_call" | custom-call | tf_op jit(solution)/shard_map/finish/pallas_call | solution.py:283
  (45 shorter events, 5.0 us)
Async XLA Ops:
  7.2 91.0 %all-gather.4.cloned.1.call-start = ((), (), s32[]{:S(2)}) async-start(), calls=%async_computation | async-start | bytes 4456448 | tf_op jit(solution)/shard_map/all_gather | solution.py:228
  7.9 126.8 %all-gather.6.cloned.1.call-start = ((), (), s32[]{:S(2)}) async-start(), calls=%async_computation.1 | async-start | bytes 4456448 | tf_op jit(solution)/shard_map/all_gather | solution.py:253
  8.9 19.4 %copy-start = (f32[128,512]{1,0:T(8,128)}, f32[128,512]{1,0:T(8,128)S(1)}, u32[]{:S(2)}) copy-start(f32[128,512]{1,0:T(8,128)S(1)} %slice_bitcast_fusion.mine) | copy-start | bytes 786436
  8.9 8.6 %collective-permute-start.10 = (f32[128,512]{1,0:T(8,128)S(1)}, f32[128,512]{1,0:T(8,128)S(1)}, u32[]{:S(2)}, u32[]{:S(2)}) collective-permute-start(f32[128,512]{1,0:T(8,128)S(1)} %slice_bitcast_fusion.mine), channel_id=1, source_target_pairs={{0,2},{1,3},{2,0},{3,1},{16,18},{17,19},{18,16},{19,17},{32,34},{3... | collective-permute-start | bytes 786440 | tf_op jit(solution)/shard_map/ppermute | solution.py:233
  13.8 13.7 %collective-permute-start = (f32[32,512]{1,0:T(8,128)}, f32[32,512]{1,0:T(8,128)S(1)}, u32[]{:S(2)}, u32[]{:S(2)}) collective-permute-start(f32[32,512]{1,0:T(8,128)} %bitcast.13), channel_id=1, source_target_pairs={{0,2},{1,3},{2,0},{3,1},{4,6},{5,7},{6,4},{7,5},{8,10},{9,11},{10,... | collective-permute-start | bytes 196616 | tf_op jit(solution)/shard_map/ppermute | solution.py:226
  17.5 10.8 %copy-start.2 = (f32[128,512]{1,0:T(8,128)}, f32[128,512]{1,0:T(8,128)S(1)}, u32[]{:S(2)}) copy-start(f32[128,512]{1,0:T(8,128)S(1)} %collective-permute-done.10.near) | copy-start | bytes 786436
  17.5 10.7 %collective-permute-start.11 = (f32[256,512]{1,0:T(8,128)S(1)}, f32[256,512]{1,0:T(8,128)S(1)}, u32[]{:S(2)}, u32[]{:S(2)}) collective-permute-start(f32[256,512]{1,0:T(8,128)S(1)} %pad_maximum_fusion), channel_id=1, source_target_pairs={{0,1},{1,0},{2,3},{3,2},{16,17},{17,16},{18,19},{19,18},{32,33},{3... | collective-permute-start | bytes 1572872 | tf_op jit(solution)/shard_map/ppermute | solution.py:238
  28.3 0.8 copy-start.1
  50.5 17.6 %collective-permute-start.1 = (f32[64,512]{1,0:T(8,128)S(1)}, f32[64,512]{1,0:T(8,128)S(1)}, u32[]{:S(2)}, u32[]{:S(2)}) collective-permute-start(f32[64,512]{1,0:T(8,128)S(1)} %pad_maximum_fusion.1), channel_id=1, source_target_pairs={{0,4},{1,5},{2,6},{3,7},{4,0},{5,1},{6,2},{7,3},{8,12},{9,13},{10,... | collective-permute-start | bytes 393224 | tf_op jit(solution)/shard_map/ppermute | solution.py:226
  52.4 15.7 %collective-permute-start.2 = (f32[64,512]{1,0:T(8,128)S(1)}, f32[64,512]{1,0:T(8,128)S(1)}, u32[]{:S(2)}, u32[]{:S(2)}) collective-permute-start(f32[64,512]{1,0:T(8,128)S(1)} %pad_maximum_fusion.1), channel_id=1, source_target_pairs={{0,8},{1,9},{2,10},{3,11},{4,12},{5,13},{6,14},{7,15},{8,0},{9,1},... | collective-permute-start | bytes 393224 | tf_op jit(solution)/shard_map/ppermute | solution.py:226
  54.4 15.8 %collective-permute-start.3 = (f32[64,512]{1,0:T(8,128)S(1)}, f32[64,512]{1,0:T(8,128)S(1)}, u32[]{:S(2)}, u32[]{:S(2)}) collective-permute-start(f32[64,512]{1,0:T(8,128)S(1)} %pad_maximum_fusion.1), channel_id=1, source_target_pairs={{0,12},{1,13},{2,14},{3,15},{4,8},{5,9},{6,10},{7,11},{8,4},{9,5},... | collective-permute-start | bytes 393224 | tf_op jit(solution)/shard_map/ppermute | solution.py:226
  70.2 4.4 %copy-start.3 = (f32[256,512]{1,0:T(8,128)}, f32[256,512]{1,0:T(8,128)S(1)}, u32[]{:S(2)}) copy-start(f32[256,512]{1,0:T(8,128)S(1)} %constant_dynamic-update-slice_fusion.own) | copy-start | bytes 1572868
  70.2 4.3 %collective-permute-start.4 = (f32[256,512]{1,0:T(8,128)S(1)}, f32[256,512]{1,0:T(8,128)S(1)}, u32[]{:S(2)}, u32[]{:S(2)}) collective-permute-start(f32[256,512]{1,0:T(8,128)S(1)} %constant_dynamic-update-slice_fusion.own), channel_id=1, source_target_pairs={{0,1},{1,0},{2,3},{3,2},{4,5},{5,4},{6,7},{7,6},{8,9},{9,8},{10,11... | collective-permute-start | bytes 1572872 | tf_op jit(solution)/shard_map/ppermute | solution.py:256
  74.5 0.9 copy-start.4
  105.1 18.0 %collective-permute-start.5 = (f32[128,512]{1,0:T(8,128)}, f32[128,512]{1,0:T(8,128)S(1)}, u32[]{:S(2)}, u32[]{:S(2)}) collective-permute-start(f32[128,512]{1,0:T(8,128)} %get-tuple-element.20), channel_id=1, source_target_pairs={{0,16},{16,0},{32,48},{48,32},{64,80},{80,64},{96,112},{112,96},{1... | collective-permute-start | bytes 786440 | tf_op jit(solution)/shard_map/ppermute | solution.py:281
  107.0 27.4 %collective-permute-start.6 = (f32[128,512]{1,0:T(8,128)}, f32[128,512]{1,0:T(8,128)S(1)}, u32[]{:S(2)}, u32[]{:S(2)}) collective-permute-start(f32[128,512]{1,0:T(8,128)} %get-tuple-element.21), channel_id=1, source_target_pairs={{0,32},{16,48},{32,0},{48,16},{64,96},{80,112},{96,64},{112,80},{1... | collective-permute-start | bytes 786440 | tf_op jit(solution)/shard_map/ppermute | solution.py:281
  111.1 23.5 %collective-permute-start.7 = (f32[128,512]{1,0:T(8,128)}, f32[128,512]{1,0:T(8,128)S(1)}, u32[]{:S(2)}, u32[]{:S(2)}) collective-permute-start(f32[128,512]{1,0:T(8,128)} %get-tuple-element.22), channel_id=1, source_target_pairs={{0,64},{16,80},{32,96},{48,112},{64,0},{80,16},{96,32},{112,48},{1... | collective-permute-start | bytes 786440 | tf_op jit(solution)/shard_map/ppermute | solution.py:281
  115.9 18.8 %collective-permute-start.8 = (f32[128,512]{1,0:T(8,128)}, f32[128,512]{1,0:T(8,128)S(1)}, u32[]{:S(2)}, u32[]{:S(2)}) collective-permute-start(f32[128,512]{1,0:T(8,128)} %get-tuple-element.23), channel_id=1, source_target_pairs={{0,128},{16,144},{32,160},{48,176},{64,192},{80,208},{96,224},{112... | collective-permute-start | bytes 786440 | tf_op jit(solution)/shard_map/ppermute | solution.py:281
  118.8 15.9 %collective-permute-start.9 = (f32[128,512]{1,0:T(8,128)}, f32[128,512]{1,0:T(8,128)S(1)}, u32[]{:S(2)}, u32[]{:S(2)}) collective-permute-start(f32[128,512]{1,0:T(8,128)} %get-tuple-element.24), channel_id=1, source_target_pairs={{0,256},{16,272},{32,288},{48,304},{64,320},{80,336},{96,352},{112... | collective-permute-start | bytes 786440 | tf_op jit(solution)/shard_map/ppermute | solution.py:281
  123.1 11.7 %copy-start.5 = (f32[128,512]{1,0:T(8,128)}, f32[128,512]{1,0:T(8,128)S(1)}, u32[]{:S(2)}) copy-start(f32[128,512]{1,0:T(8,128)S(1)} %collective-permute-done.5.r0) | copy-start | bytes 786436
  134.4 0.7 copy-start.6
  134.7 0.7 copy-start.7
  134.7 0.8 copy-start.8
  134.7 0.9 copy-start.9
Sparse Core Ops, SparseCore 0:
  10.1 54.1 all-gather.3
  66.4 49.5 all-gather.5
where the time goes:
time: 148 us; the launch traced here: 147 us
  Pallas kernels  55.6 us (38%)
  starting transfers between devices  47.6 us (32%)
  waiting for transfers between devices  22.9 us (15%)
  between operations  14.3 us (10%)
  local copies, waits for them, and re-layouts  3.58 us (2%)
  other arithmetic  3.08 us (2%)
    pallas_call x1, Pallas kernels, per_device(): pl.pallas_call(child_kernel, out_shape=(shape(slab, n), shape(BLK, n), sh...  22.8 us
    pallas_call x1, Pallas kernels, per_device(): pl.pallas_call(anc_kernel, grid=(1,), out_shape=(shape(BLK, n),) * 2, in_...  21.4 us
    ppermute x5, starting transfers between devices, per_device(): arrived[level] = lax.ppermute(messages[level], 'leaf', pairs)  17.9 us
    ppermute x4, starting transfers between devices, pair_up(): return lax.ppermute(value, 'front', pairs)  13.3 us
    ppermute x5, waiting for transfers between devices, per_device(): arrived[level] = lax.ppermute(messages[level], 'leaf', pairs)  11.6 us
    ppermute x1, starting transfers between devices, per_device(): lax.ppermute(jnp.concatenate([top, near], 0), 'front', [(f, f ^ 1) for f...  8.44 us
    ppermute x4, waiting for transfers between devices, pair_up(): return lax.ppermute(value, 'front', pairs)  8.22 us
    pallas_call x1, Pallas kernels, per_device(): pl.pallas_call(update_kernel, out_shape=(shape(BLK, n),) * levels, in_spe...  6.88 us
  transfers between devices with their start and end apart: 14, of which 6 were waited for; matrix products, arithmetic and copies ran while one was open for 3% of the time, Pallas kernels for 35%

commit v1 on v0

--- a/solution.py
+++ b/solution.py
@@ -1,3 +1,5 @@
+import functools
+
 import jax
 import jax.numpy as jnp
 from jax import lax
@@ -145,19 +147,36 @@
     inv_out[...] = x_ref[pl.ds(at, BLK), :]
 
 
-def update_kernel(info, w, panels, m0, m1, m2, m3, m4, u_ref, table):
-    outs = (m0, m1, m2, m3, m4)
-    wide = m0.shape[1] // BLK
-    fronts = panels.shape[0]
-    for i in range(len(outs) * wide):
+def halves(x):
+    high = x.astype(jnp.bfloat16)
+    return high, (x - high.astype(F32)).astype(jnp.bfloat16)
+
+
+def dot_halves(a, b):
+    def part(x, y):
+        return lax.dot_general(x, y, (((1,), (1,)), ((), ())), preferred_element_type=F32)
+
+    return part(a[0], b[0]) + (part(a[0], b[1]) + part(a[1], b[0]))
+
+
+def block_table(info, table, wide, levels, fronts):
+    for i in range(levels * wide):
         table[i] = -1
     for j in range(fronts):
         diff = info[2 + j] ^ info[0]
-        level = sum((diff >= 2**b).astype(jnp.int32) for b in range(1, len(outs)))
+        level = sum((diff >= 2**b).astype(jnp.int32) for b in range(1, levels))
         table[level * wide + info[2 + fronts + j]] = j
+
+
+def update_kernel(chosen, levels, info, w, panels, *refs):
+    outs, (table, u_ref) = refs[: len(chosen)], refs[len(chosen) :]
+    wide = outs[0].shape[1] // BLK
+    fronts = panels.shape[0]
+    block_table(info, table, wide, levels, fronts)
+    left = halves(w[...])
     for j in range(fronts):
-        u_ref[j] = dot(w[...], panels[j], 1, 1)
-    for level, out in enumerate(outs):
+        u_ref[j] = dot_halves(left, halves(panels[j]))
+    for level, out in zip(chosen, outs):
         for c in range(wide):
             j = table[level * wide + c]
             out[:, BLK * c : BLK * (c + 1)] = jnp.where(j >= 0, u_ref[jnp.maximum(j, 0)], 0.0)
@@ -171,8 +190,8 @@
     n = t.shape[1]
     half = n // 2
     x = x_ref[...].reshape(n, n)
-    out[:, :half] = dot(t[:, :half], x[:half, :half], 1, 1)
-    out[:, half:] = dot(t[...], x[half:, :], 1, 1)
+    out[:, :half] = dot_halves(halves(t[:, :half]), halves(x[:half, :half]))
+    out[:, half:] = dot_halves(halves(t[...]), halves(x[half:, :]))
 
     @pl.when(info[1] < t.shape[1] // BLK)
     def _():
@@ -263,17 +282,19 @@
         name="child_cholesky",
     )(info, own, other, child_panel[0])
 
-    messages = pl.pallas_call(
-        update_kernel,
-        out_shape=(shape(BLK, n),) * levels,
+    table = pltpu.SMEM((levels * (n // BLK),), jnp.int32)
+    messages = [None] * levels
+    chosen = (2, 1, 4, 3, 0)
+    others = pl.pallas_call(
+        functools.partial(update_kernel, chosen, levels),
+        out_shape=(shape(BLK, n),) * len(chosen),
         in_specs=[SMEM, VMEM, VMEM],
-        out_specs=(VMEM,) * levels,
-        scratch_shapes=[
-            pltpu.VMEM((fronts, BLK, BLK), F32),
-            pltpu.SMEM((levels * (n // BLK),), jnp.int32),
-        ],
+        out_specs=(VMEM,) * len(chosen),
+        scratch_shapes=[table, pltpu.VMEM((fronts, BLK, BLK), F32)],
         name="update",
     )(info, w, gathered)
+    for level, message in zip(chosen, others):
+        messages[level] = message
 
     arrived = [None] * levels
     for level in (2, 4, 1, 3, 0):

time: 148 us -> 146 us (0.986)
  Pallas kernels: 55.6 us -> 53.4 us
    pallas_call x1, Pallas kernels: 6.88 us -> 5.25 us  [per_device(): pl.pallas_call(functools.partial(update_kernel, chosen, levels), out_shap...]
  transfers between devices with their start and end apart: 14 -> 14, of which waited for: 6 -> 6; matrix products, arithmetic and copies ran while one was open for 3% -> 3% of each run, Pallas kernels for 35% -> 34%
where the time goes in v1:
time: 146 us; the launch traced here: 145 us
  Pallas kernels  53.4 us (37%)
  starting transfers between devices  47.6 us (33%)
  waiting for transfers between devices  22.9 us (16%)
  between operations  14.3 us (10%)
  local copies, waits for them, and re-layouts  3.58 us (2%)
  other arithmetic  3.08 us (2%)
    pallas_call x1, Pallas kernels, per_device(): pl.pallas_call(child_kernel, out_shape=(shape(slab, n), shape(BLK, n), sh...  22.8 us
    pallas_call x1, Pallas kernels, per_device(): pl.pallas_call(anc_kernel, grid=(1,), out_shape=(shape(BLK, n),) * 2, in_...  21.4 us
    ppermute x5, starting transfers between devices, per_device(): arrived[level] = lax.ppermute(messages[level], 'leaf', pairs)  17.9 us
    ppermute x4, starting transfers between devices, pair_up(): return lax.ppermute(value, 'front', pairs)  13.3 us
    ppermute x5, waiting for transfers between devices, per_device(): arrived[level] = lax.ppermute(messages[level], 'leaf', pairs)  11.6 us
    ppermute x1, starting transfers between devices, per_device(): lax.ppermute(jnp.concatenate([top, near], 0), 'front', [(f, f ^ 1) for f...  8.44 us
    ppermute x4, waiting for transfers between devices, pair_up(): return lax.ppermute(value, 'front', pairs)  8.22 us
    pallas_call x1, Pallas kernels, per_device(): pl.pallas_call(functools.partial(update_kernel, chosen, levels), out_shap...  5.25 us
  transfers between devices with their start and end apart: 14, of which 6 were waited for; matrix products, arithmetic and copies ran while one was open for 3% of the time, Pallas kernels for 34%

profile of v1, /device:TPU:1, one launch (start us, length us, event | category | flops | bytes accessed | tf_op | source)
XLA Modules:
  0.0 144.8 jit_solution(16035929267802365485)
XLA Ops:
  7.9 1.0 slice_bitcast_fusion.mine
  8.9 4.8 %collective-permute-start.10 = (f32[128,512]{1,0:T(8,128)S(1)}, f32[128,512]{1,0:T(8,128)S(1)}, u32[]{:S(2)}, u32[]{:S(2)}) collective-permute-start(f32[128,512]{1,0:T(8,128)S(1)} %slice_bitcast_fusion.mine), channel_id=1, source_target_pairs={{0,2},{1,3},{2,0},{3,1},{16,18},{17,19},{18,16},{19,17},{32,34},{3... | collective-permute-start | bytes 786440 | tf_op jit(solution)/shard_map/ppermute | solution.py:252
  13.8 1.9 %collective-permute-start = (f32[32,512]{1,0:T(8,128)}, f32[32,512]{1,0:T(8,128)S(1)}, u32[]{:S(2)}, u32[]{:S(2)}) collective-permute-start(f32[32,512]{1,0:T(8,128)} %bitcast.13), channel_id=1, source_target_pairs={{0,2},{1,3},{2,0},{3,1},{4,6},{5,7},{6,4},{7,5},{8,10},{9,11},{10,... | collective-permute-start | bytes 196616 | tf_op jit(solution)/shard_map/ppermute | solution.py:245
  16.5 1.0 collective-permute-done.10.near
  17.5 8.4 %collective-permute-start.11 = (f32[256,512]{1,0:T(8,128)S(1)}, f32[256,512]{1,0:T(8,128)S(1)}, u32[]{:S(2)}, u32[]{:S(2)}) collective-permute-start(f32[256,512]{1,0:T(8,128)S(1)} %pad_maximum_fusion), channel_id=1, source_target_pairs={{0,1},{1,0},{2,3},{3,2},{16,17},{17,16},{18,19},{19,18},{32,33},{3... | collective-permute-start | bytes 1572872 | tf_op jit(solution)/shard_map/ppermute | solution.py:257
  26.0 0.9 fusion
  29.1 21.4 %ancestor_cholesky.1 = (f32[128,512]{1,0:T(8,128)}, f32[128,512]{1,0:T(8,128)}) custom-call(s32[39]{0:T(128)} %compare_select_fusion.2.info, f32[128,512]{1,0:T(8,128)} %copy-done, f32[128,512]{1,0:T(8,128)} %copy-done.2, f32[256,512]{1,0:T(8,128)} %copy-done.1, f32[256,512]{1,0:T(8,128)} %copy-done.1), custom_call_target="tpu_custom_call" | custom-call | tf_op jit(solution)/shard_map/ancestor_cholesky/pallas_call | solution.py:262
  50.5 1.9 %collective-permute-start.1 = (f32[64,512]{1,0:T(8,128)S(1)}, f32[64,512]{1,0:T(8,128)S(1)}, u32[]{:S(2)}, u32[]{:S(2)}) collective-permute-start(f32[64,512]{1,0:T(8,128)S(1)} %pad_maximum_fusion.1), channel_id=1, source_target_pairs={{0,4},{1,5},{2,6},{3,7},{4,0},{5,1},{6,2},{7,3},{8,12},{9,13},{10,... | collective-permute-start | bytes 393224 | tf_op jit(solution)/shard_map/ppermute | solution.py:245
  52.4 1.9 %collective-permute-start.2 = (f32[64,512]{1,0:T(8,128)S(1)}, f32[64,512]{1,0:T(8,128)S(1)}, u32[]{:S(2)}, u32[]{:S(2)}) collective-permute-start(f32[64,512]{1,0:T(8,128)S(1)} %pad_maximum_fusion.1), channel_id=1, source_target_pairs={{0,8},{1,9},{2,10},{3,11},{4,12},{5,13},{6,14},{7,15},{8,0},{9,1},... | collective-permute-start | bytes 393224 | tf_op jit(solution)/shard_map/ppermute | solution.py:245
  54.4 7.5 %collective-permute-start.3 = (f32[64,512]{1,0:T(8,128)S(1)}, f32[64,512]{1,0:T(8,128)S(1)}, u32[]{:S(2)}, u32[]{:S(2)}) collective-permute-start(f32[64,512]{1,0:T(8,128)S(1)} %pad_maximum_fusion.1), channel_id=1, source_target_pairs={{0,12},{1,13},{2,14},{3,15},{4,8},{5,9},{6,10},{7,11},{8,4},{9,5},... | collective-permute-start | bytes 393224 | tf_op jit(solution)/shard_map/ppermute | solution.py:245
  61.9 6.2 %collective-permute-done.1 = f32[64,512]{1,0:T(8,128)S(1)} collective-permute-done((f32[64,512]{1,0:T(8,128)S(1)}, f32[64,512]{1,0:T(8,128)S(1)}, u32[]{:S(2)}, u32[]{:S(2)}) %collective-permute-start.1) | collective-permute-done | bytes 131104 | tf_op jit(solution)/shard_map/ppermute | solution.py:245
  68.1 2.0 %collective-permute-done.3 = f32[64,512]{1,0:T(8,128)S(1)} collective-permute-done((f32[64,512]{1,0:T(8,128)S(1)}, f32[64,512]{1,0:T(8,128)S(1)}, u32[]{:S(2)}, u32[]{:S(2)}) %collective-permute-start.3) | collective-permute-done | bytes 131104 | tf_op jit(solution)/shard_map/ppermute | solution.py:245
  70.2 3.0 %collective-permute-start.4 = (f32[256,512]{1,0:T(8,128)S(1)}, f32[256,512]{1,0:T(8,128)S(1)}, u32[]{:S(2)}, u32[]{:S(2)}) collective-permute-start(f32[256,512]{1,0:T(8,128)S(1)} %constant_dynamic-update-slice_fusion.own), channel_id=1, source_target_pairs={{0,1},{1,0},{2,3},{3,2},{4,5},{5,4},{6,7},{7,6},{8,9},{9,8},{10,11... | collective-permute-start | bytes 1572872 | tf_op jit(solution)/shard_map/ppermute | solution.py:275
  73.2 1.3 collective-permute-done.4.other
  74.5 0.9 copy-done.4
  75.4 22.8 %child_cholesky.1 = (f32[32,512]{1,0:T(8,128)}, f32[128,512]{1,0:T(8,128)}, f32[128,512]{1,0:T(8,128)}) custom-call(s32[39]{0:T(128)} %compare_select_fusion.2.info, f32[256,512]{1,0:T(8,128)} %copy-done.3, f32[256,512]{1,0:T(8,128)} %copy-done.4, f32[128,512]{1,0:T(8,128)} %bitcast.12), custom_call_target="tpu_custom_call" | custom-call | tf_op jit(solution)/shard_map/child_cholesky/pallas_call | solution.py:276
  98.2 5.2 %update.1 = (f32[128,512]{1,0:T(8,128)}, f32[128,512]{1,0:T(8,128)}, f32[128,512]{1,0:T(8,128)}, f32[128,512]{1,0:T(8,128)}, f32[128,512]{1,0:T(8,128)}) custom-call(s32[39]{0:T(128)} %compare_select_fusion.2.info, f32[128,512]{1,0:T(8,128)} %get-tuple-element.19.w, f32[16,128,512]{2,1,0:T(8,128)} %all-gather.4.cloned.1.call-done.panels), custom_call_target="tpu_custom_call" | custom-call | tf_op jit(solution)/shard_map/update/pallas_call | solution.py:288
  103.5 1.9 %collective-permute-start.5 = (f32[128,512]{1,0:T(8,128)}, f32[128,512]{1,0:T(8,128)S(1)}, u32[]{:S(2)}, u32[]{:S(2)}) collective-permute-start(f32[128,512]{1,0:T(8,128)} %get-tuple-element.20), channel_id=1, source_target_pairs={{0,16},{16,0},{32,48},{48,32},{64,80},{80,64},{96,112},{112,96},{1... | collective-permute-start | bytes 786440 | tf_op jit(solution)/shard_map/ppermute | solution.py:302
  105.4 4.1 %collective-permute-start.6 = (f32[128,512]{1,0:T(8,128)}, f32[128,512]{1,0:T(8,128)S(1)}, u32[]{:S(2)}, u32[]{:S(2)}) collective-permute-start(f32[128,512]{1,0:T(8,128)} %get-tuple-element.21), channel_id=1, source_target_pairs={{0,32},{16,48},{32,0},{48,16},{64,96},{80,112},{96,64},{112,80},{1... | collective-permute-start | bytes 786440 | tf_op jit(solution)/shard_map/ppermute | solution.py:302
  109.5 4.7 %collective-permute-start.7 = (f32[128,512]{1,0:T(8,128)}, f32[128,512]{1,0:T(8,128)S(1)}, u32[]{:S(2)}, u32[]{:S(2)}) collective-permute-start(f32[128,512]{1,0:T(8,128)} %get-tuple-element.22), channel_id=1, source_target_pairs={{0,64},{16,80},{32,96},{48,112},{64,0},{80,16},{96,32},{112,48},{1... | collective-permute-start | bytes 786440 | tf_op jit(solution)/shard_map/ppermute | solution.py:302
  114.2 3.0 %collective-permute-start.8 = (f32[128,512]{1,0:T(8,128)}, f32[128,512]{1,0:T(8,128)S(1)}, u32[]{:S(2)}, u32[]{:S(2)}) collective-permute-start(f32[128,512]{1,0:T(8,128)} %get-tuple-element.23), channel_id=1, source_target_pairs={{0,128},{16,144},{32,160},{48,176},{64,192},{80,208},{96,224},{112... | collective-permute-start | bytes 786440 | tf_op jit(solution)/shard_map/ppermute | solution.py:302
  117.2 4.2 %collective-permute-start.9 = (f32[128,512]{1,0:T(8,128)}, f32[128,512]{1,0:T(8,128)S(1)}, u32[]{:S(2)}, u32[]{:S(2)}) collective-permute-start(f32[128,512]{1,0:T(8,128)} %get-tuple-element.24), channel_id=1, source_target_pairs={{0,256},{16,272},{32,288},{48,304},{64,320},{80,336},{96,352},{112... | collective-permute-start | bytes 786440 | tf_op jit(solution)/shard_map/ppermute | solution.py:302
  121.4 11.3 %collective-permute-done.6.r1 = f32[128,512]{1,0:T(8,128)S(1)} collective-permute-done((f32[128,512]{1,0:T(8,128)}, f32[128,512]{1,0:T(8,128)S(1)}, u32[]{:S(2)}, u32[]{:S(2)}) %collective-permute-start.6) | collective-permute-done | bytes 262176 | tf_op jit(solution)/shard_map/ppermute | solution.py:302
  134.0 4.0 %finish.1 = f32[512,512]{1,0:T(8,128)} custom-call(s32[39]{0:T(128)} %compare_select_fusion.2.info, f32[512,512]{1,0:T(8,128)} %bitcast.10, f32[128,512]{1,0:T(8,128)} %copy-done.5, f32[128,512]{1,0:T(8,128)} %copy-done.6, f32[128,512]{1,0:T(8,128)} %copy-done.7, f32[128,512]{1,0:T(8,128)} %copy-done.8, f32[128,512]{1,0:T(8,128)} %copy-done.9, ...), custom_call_target="tpu_custom_call" | custom-call | tf_op jit(solution)/shard_map/finish/pallas_call | solution.py:304
  (45 shorter events, 5.0 us)
Async XLA Ops:
  7.2 91.0 %all-gather.4.cloned.1.call-start = ((), (), s32[]{:S(2)}) async-start(), calls=%async_computation | async-start | bytes 4456448 | tf_op jit(solution)/shard_map/all_gather | solution.py:247
  7.9 125.2 %all-gather.6.cloned.1.call-start = ((), (), s32[]{:S(2)}) async-start(), calls=%async_computation.1 | async-start | bytes 4456448 | tf_op jit(solution)/shard_map/all_gather | solution.py:272
  8.9 19.4 %copy-start = (f32[128,512]{1,0:T(8,128)}, f32[128,512]{1,0:T(8,128)S(1)}, u32[]{:S(2)}) copy-start(f32[128,512]{1,0:T(8,128)S(1)} %slice_bitcast_fusion.mine) | copy-start | bytes 786436
  8.9 8.6 %collective-permute-start.10 = (f32[128,512]{1,0:T(8,128)S(1)}, f32[128,512]{1,0:T(8,128)S(1)}, u32[]{:S(2)}, u32[]{:S(2)}) collective-permute-start(f32[128,512]{1,0:T(8,128)S(1)} %slice_bitcast_fusion.mine), channel_id=1, source_target_pairs={{0,2},{1,3},{2,0},{3,1},{16,18},{17,19},{18,16},{19,17},{32,34},{3... | collective-permute-start | bytes 786440 | tf_op jit(solution)/shard_map/ppermute | solution.py:252
  13.8 13.7 %collective-permute-start = (f32[32,512]{1,0:T(8,128)}, f32[32,512]{1,0:T(8,128)S(1)}, u32[]{:S(2)}, u32[]{:S(2)}) collective-permute-start(f32[32,512]{1,0:T(8,128)} %bitcast.13), channel_id=1, source_target_pairs={{0,2},{1,3},{2,0},{3,1},{4,6},{5,7},{6,4},{7,5},{8,10},{9,11},{10,... | collective-permute-start | bytes 196616 | tf_op jit(solution)/shard_map/ppermute | solution.py:245
  17.5 10.8 %copy-start.2 = (f32[128,512]{1,0:T(8,128)}, f32[128,512]{1,0:T(8,128)S(1)}, u32[]{:S(2)}) copy-start(f32[128,512]{1,0:T(8,128)S(1)} %collective-permute-done.10.near) | copy-start | bytes 786436
  17.5 10.7 %collective-permute-start.11 = (f32[256,512]{1,0:T(8,128)S(1)}, f32[256,512]{1,0:T(8,128)S(1)}, u32[]{:S(2)}, u32[]{:S(2)}) collective-permute-start(f32[256,512]{1,0:T(8,128)S(1)} %pad_maximum_fusion), channel_id=1, source_target_pairs={{0,1},{1,0},{2,3},{3,2},{16,17},{17,16},{18,19},{19,18},{32,33},{3... | collective-permute-start | bytes 1572872 | tf_op jit(solution)/shard_map/ppermute | solution.py:257
  28.3 0.8 copy-start.1
  50.5 17.6 %collective-permute-start.1 = (f32[64,512]{1,0:T(8,128)S(1)}, f32[64,512]{1,0:T(8,128)S(1)}, u32[]{:S(2)}, u32[]{:S(2)}) collective-permute-start(f32[64,512]{1,0:T(8,128)S(1)} %pad_maximum_fusion.1), channel_id=1, source_target_pairs={{0,4},{1,5},{2,6},{3,7},{4,0},{5,1},{6,2},{7,3},{8,12},{9,13},{10,... | collective-permute-start | bytes 393224 | tf_op jit(solution)/shard_map/ppermute | solution.py:245
  52.4 15.7 %collective-permute-start.2 = (f32[64,512]{1,0:T(8,128)S(1)}, f32[64,512]{1,0:T(8,128)S(1)}, u32[]{:S(2)}, u32[]{:S(2)}) collective-permute-start(f32[64,512]{1,0:T(8,128)S(1)} %pad_maximum_fusion.1), channel_id=1, source_target_pairs={{0,8},{1,9},{2,10},{3,11},{4,12},{5,13},{6,14},{7,15},{8,0},{9,1},... | collective-permute-start | bytes 393224 | tf_op jit(solution)/shard_map/ppermute | solution.py:245
  54.4 15.8 %collective-permute-start.3 = (f32[64,512]{1,0:T(8,128)S(1)}, f32[64,512]{1,0:T(8,128)S(1)}, u32[]{:S(2)}, u32[]{:S(2)}) collective-permute-start(f32[64,512]{1,0:T(8,128)S(1)} %pad_maximum_fusion.1), channel_id=1, source_target_pairs={{0,12},{1,13},{2,14},{3,15},{4,8},{5,9},{6,10},{7,11},{8,4},{9,5},... | collective-permute-start | bytes 393224 | tf_op jit(solution)/shard_map/ppermute | solution.py:245
  70.2 4.4 %copy-start.3 = (f32[256,512]{1,0:T(8,128)}, f32[256,512]{1,0:T(8,128)S(1)}, u32[]{:S(2)}) copy-start(f32[256,512]{1,0:T(8,128)S(1)} %constant_dynamic-update-slice_fusion.own) | copy-start | bytes 1572868
  70.2 4.3 %collective-permute-start.4 = (f32[256,512]{1,0:T(8,128)S(1)}, f32[256,512]{1,0:T(8,128)S(1)}, u32[]{:S(2)}, u32[]{:S(2)}) collective-permute-start(f32[256,512]{1,0:T(8,128)S(1)} %constant_dynamic-update-slice_fusion.own), channel_id=1, source_target_pairs={{0,1},{1,0},{2,3},{3,2},{4,5},{5,4},{6,7},{7,6},{8,9},{9,8},{10,11... | collective-permute-start | bytes 1572872 | tf_op jit(solution)/shard_map/ppermute | solution.py:275
  74.5 0.9 copy-start.4
  103.5 18.0 %collective-permute-start.5 = (f32[128,512]{1,0:T(8,128)}, f32[128,512]{1,0:T(8,128)S(1)}, u32[]{:S(2)}, u32[]{:S(2)}) collective-permute-start(f32[128,512]{1,0:T(8,128)} %get-tuple-element.20), channel_id=1, source_target_pairs={{0,16},{16,0},{32,48},{48,32},{64,80},{80,64},{96,112},{112,96},{1... | collective-permute-start | bytes 786440 | tf_op jit(solution)/shard_map/ppermute | solution.py:302
  105.4 27.4 %collective-permute-start.6 = (f32[128,512]{1,0:T(8,128)}, f32[128,512]{1,0:T(8,128)S(1)}, u32[]{:S(2)}, u32[]{:S(2)}) collective-permute-start(f32[128,512]{1,0:T(8,128)} %get-tuple-element.21), channel_id=1, source_target_pairs={{0,32},{16,48},{32,0},{48,16},{64,96},{80,112},{96,64},{112,80},{1... | collective-permute-start | bytes 786440 | tf_op jit(solution)/shard_map/ppermute | solution.py:302
  109.5 23.5 %collective-permute-start.7 = (f32[128,512]{1,0:T(8,128)}, f32[128,512]{1,0:T(8,128)S(1)}, u32[]{:S(2)}, u32[]{:S(2)}) collective-permute-start(f32[128,512]{1,0:T(8,128)} %get-tuple-element.22), channel_id=1, source_target_pairs={{0,64},{16,80},{32,96},{48,112},{64,0},{80,16},{96,32},{112,48},{1... | collective-permute-start | bytes 786440 | tf_op jit(solution)/shard_map/ppermute | solution.py:302
  114.2 18.8 %collective-permute-start.8 = (f32[128,512]{1,0:T(8,128)}, f32[128,512]{1,0:T(8,128)S(1)}, u32[]{:S(2)}, u32[]{:S(2)}) collective-permute-start(f32[128,512]{1,0:T(8,128)} %get-tuple-element.23), channel_id=1, source_target_pairs={{0,128},{16,144},{32,160},{48,176},{64,192},{80,208},{96,224},{112... | collective-permute-start | bytes 786440 | tf_op jit(solution)/shard_map/ppermute | solution.py:302
  117.2 15.9 %collective-permute-start.9 = (f32[128,512]{1,0:T(8,128)}, f32[128,512]{1,0:T(8,128)S(1)}, u32[]{:S(2)}, u32[]{:S(2)}) collective-permute-start(f32[128,512]{1,0:T(8,128)} %get-tuple-element.24), channel_id=1, source_target_pairs={{0,256},{16,272},{32,288},{48,304},{64,320},{80,336},{96,352},{112... | collective-permute-start | bytes 786440 | tf_op jit(solution)/shard_map/ppermute | solution.py:302
  121.4 11.7 %copy-start.5 = (f32[128,512]{1,0:T(8,128)}, f32[128,512]{1,0:T(8,128)S(1)}, u32[]{:S(2)}) copy-start(f32[128,512]{1,0:T(8,128)S(1)} %collective-permute-done.5.r0) | copy-start | bytes 786436
  132.8 0.7 copy-start.6
  133.0 0.7 copy-start.7
  133.0 0.8 copy-start.8
  133.0 0.9 copy-start.9
Sparse Core Ops, SparseCore 0:
  10.1 54.1 all-gather.3
  66.4 49.5 all-gather.5

commit v2 on v1

--- a/solution.py
+++ b/solution.py
@@ -137,8 +137,8 @@
     w_out[:, half:] = dot(second, x_ref[half:, half:])
 
 
-def anc_kernel(info, mine, near, across0, across1, rows_out, inv_out, t, l_ref, x_ref, m_ref):
-    own = jnp.minimum(info[1], t.shape[0] // BLK - 1)
+def anc_kernel(place, mine, near, across0, across1, rows_out, inv_out, t, l_ref, x_ref, m_ref):
+    own = jnp.minimum(place[0], t.shape[0] // BLK - 1)
     for part, mask in ((mine, 0), (near, 2), (across0, 1), (across1, 3)):
         t[pl.ds(pl.multiple_of((own ^ mask) * BLK, BLK), BLK), :] = part[...]
     factor(t, l_ref, x_ref, m_ref)
@@ -238,7 +238,7 @@
     n = child_panel.shape[2]
     levels = lax.axis_size("leaf").bit_length() - 1
 
-    info = make_info(group, front, levels, dest_list, col_list, row_list)
+    place = jnp.full((1,), front, jnp.int32)
 
     def pair_up(value, partner):
         pairs = [(2 * z + c, 2 * partner(z) + c) for z in range(fronts // 2) for c in range(2)]
@@ -247,10 +247,10 @@
     gathered = lax.all_gather(child_panel[0], "front", axis=0, tiled=False)
 
     mine = child_pivot[0]
-    pair = jnp.concatenate([mine, pair_up(mine, lambda z: z ^ 1)], 0)
+    beside = pair_up(mine, lambda z: z ^ 1)
+    pair = jnp.concatenate([mine, beside], 0)
     top = anc_front[0, 0, :BLK]
     near = lax.ppermute(top, "front", [(f, f ^ 2) for f in range(n // BLK)])
-    pair, info = lax.optimization_barrier((pair, info))
     parts = [pair]
     for k in (2, 4, 6):
         parts.append(pair_up(pair, lambda z, k=k: z ^ k))
@@ -268,11 +268,15 @@
         out_specs=(VMEM, VMEM),
         scratch_shapes=[square, square, square, work],
         name="ancestor_cholesky",
-    )(info, top, near, across, across)
+    )(place, top, near, across, across)
     inverses = lax.all_gather(anc_inv, "front", axis=0, tiled=False)
 
     own = jnp.concatenate(parts, 0)
+    own, dest_list, col_list, row_list = lax.optimization_barrier(
+        (own, dest_list, col_list, row_list)
+    )
     other = lax.ppermute(own, "front", [(f, f ^ 1) for f in range(fronts)])
+    info = make_info(group, front, levels, dest_list, col_list, row_list)
     lower_rows, panel, w = pl.pallas_call(
         child_kernel,
         out_shape=(shape(slab, n), shape(BLK, n), shape(BLK, n)),

time: 146 us -> 153 us (1.048)
  waiting for transfers between devices: 22.9 us -> 30.2 us
    ppermute x4, waiting for transfers between devices: 8.22 us -> 11.3 us  [pair_up(): return lax.ppermute(value, 'front', pairs)]
    ppermute x1, waiting for transfers between devices: 0.99 us -> 3.75 us  [per_device(): near = lax.ppermute(top, 'front', [(f, f ^ 2) for f in range(n // BLK)])]
    unnamed x23 -> x30, local copies, waits for them, and re-layouts: 2.59 us -> 3.52 us
  transfers between devices with their start and end apart: 14 -> 14, of which waited for: 6 -> 7; matrix products, arithmetic and copies ran while one was open for 3% -> 2% of each run, Pallas kernels for 34% -> 33%
where the time goes in v2:
time: 153 us; the launch traced here: 151 us
  Pallas kernels  53.2 us (35%)
  starting transfers between devices  46.7 us (31%)
  waiting for transfers between devices  30.2 us (20%)
  between operations  14.3 us (9%)
  local copies, waits for them, and re-layouts  4.52 us (3%)
  other arithmetic  1.72 us (1%)
    pallas_call x1, Pallas kernels, per_device(): pl.pallas_call(child_kernel, out_shape=(shape(slab, n), shape(BLK, n), sh...  22.8 us
    pallas_call x1, Pallas kernels, per_device(): pl.pallas_call(anc_kernel, grid=(1,), out_shape=(shape(BLK, n),) * 2, in_...  21.2 us
    ppermute x5, starting transfers between devices, per_device(): arrived[level] = lax.ppermute(messages[level], 'leaf', pairs)  16.8 us
    ppermute x4, starting transfers between devices, pair_up(): return lax.ppermute(value, 'front', pairs)  13.3 us
    ppermute x5, waiting for transfers between devices, per_device(): arrived[level] = lax.ppermute(messages[level], 'leaf', pairs)  12.4 us
    ppermute x4, waiting for transfers between devices, pair_up(): return lax.ppermute(value, 'front', pairs)  11.3 us
    ppermute x1, starting transfers between devices, per_device(): lax.ppermute(jnp.concatenate([top, near], 0), 'front', [(f, f ^ 1) for f...  8.44 us
    pallas_call x1, Pallas kernels, per_device(): pl.pallas_call(functools.partial(update_kernel, chosen, levels), out_shap...  5.21 us
  transfers between devices with their start and end apart: 14, of which 7 were waited for; matrix products, arithmetic and copies ran while one was open for 2% of the time, Pallas kernels for 33%

profile of v2, /device:TPU:1, one launch (start us, length us, event | category | flops | bytes accessed | tf_op | source)
XLA Modules:
  0.0 150.7 jit_solution(13876108311151028376)
XLA Ops:
  8.0 1.0 slice_bitcast_fusion.mine
  9.0 4.8 %collective-permute-start.10 = (f32[128,512]{1,0:T(8,128)S(1)}, f32[128,512]{1,0:T(8,128)S(1)}, u32[]{:S(2)}, u32[]{:S(2)}) collective-permute-start(f32[128,512]{1,0:T(8,128)S(1)} %slice_bitcast_fusion.mine), channel_id=1, source_target_pairs={{0,2},{1,3},{2,0},{3,1},{16,18},{17,19},{18,16},{19,17},{32,34},{3... | collective-permute-start | bytes 786440 | tf_op jit(solution)/shard_map/ppermute | solution.py:253
  13.8 3.7 %collective-permute-done.10.near = f32[128,512]{1,0:T(8,128)S(1)} collective-permute-done((f32[128,512]{1,0:T(8,128)S(1)}, f32[128,512]{1,0:T(8,128)S(1)}, u32[]{:S(2)}, u32[]{:S(2)}) %collective-permute-start.10) | collective-permute-done | bytes 262176 | tf_op jit(solution)/shard_map/ppermute | solution.py:253
  17.6 8.4 %collective-permute-start.11 = (f32[256,512]{1,0:T(8,128)S(1)}, f32[256,512]{1,0:T(8,128)S(1)}, u32[]{:S(2)}, u32[]{:S(2)}) collective-permute-start(f32[256,512]{1,0:T(8,128)S(1)} %pad_maximum_fusion), channel_id=1, source_target_pairs={{0,1},{1,0},{2,3},{3,2},{16,17},{17,16},{18,19},{19,18},{32,33},{3... | collective-permute-start | bytes 1572872 | tf_op jit(solution)/shard_map/ppermute | solution.py:257
  26.0 1.5 %collective-permute-done.11.across0.across1 = f32[256,512]{1,0:T(8,128)S(1)} collective-permute-done((f32[256,512]{1,0:T(8,128)S(1)}, f32[256,512]{1,0:T(8,128)S(1)}, u32[]{:S(2)}, u32[]{:S(2)}) %collective-permute-start.11) | collective-permute-done | bytes 524320 | tf_op jit(solution)/shard_map/ppermute | solution.py:257
  28.3 21.2 %ancestor_cholesky.1 = (f32[128,512]{1,0:T(8,128)}, f32[128,512]{1,0:T(8,128)}) custom-call(s32[1]{0:T(128)} %bitcast.5.place, f32[128,512]{1,0:T(8,128)} %copy-done, f32[128,512]{1,0:T(8,128)} %copy-done.2, f32[256,512]{1,0:T(8,128)} %copy-done.1, f32[256,512]{1,0:T(8,128)} %copy-done.1), custom_call_target="tpu_custom_call" | custom-call | tf_op jit(solution)/shard_map/ancestor_cholesky/pallas_call | solution.py:262
  49.6 1.9 %collective-permute-start = (f32[32,512]{1,0:T(8,128)}, f32[32,512]{1,0:T(8,128)S(1)}, u32[]{:S(2)}, u32[]{:S(2)}) collective-permute-start(f32[32,512]{1,0:T(8,128)} %bitcast.15), channel_id=1, source_target_pairs={{0,2},{1,3},{2,0},{3,1},{4,6},{5,7},{6,4},{7,5},{8,10},{9,11},{10,... | collective-permute-start | bytes 196616 | tf_op jit(solution)/shard_map/ppermute | solution.py:245
  52.4 4.5 %collective-permute-done = f32[32,512]{1,0:T(8,128)S(1)} collective-permute-done((f32[32,512]{1,0:T(8,128)}, f32[32,512]{1,0:T(8,128)S(1)}, u32[]{:S(2)}, u32[]{:S(2)}) %collective-permute-start) | collective-permute-done | bytes 65568 | tf_op jit(solution)/shard_map/ppermute | solution.py:245
  57.7 1.9 %collective-permute-start.1 = (f32[64,512]{1,0:T(8,128)S(1)}, f32[64,512]{1,0:T(8,128)S(1)}, u32[]{:S(2)}, u32[]{:S(2)}) collective-permute-start(f32[64,512]{1,0:T(8,128)S(1)} %pad_maximum_fusion.1), channel_id=1, source_target_pairs={{0,4},{1,5},{2,6},{3,7},{4,0},{5,1},{6,2},{7,3},{8,12},{9,13},{10,... | collective-permute-start | bytes 393224 | tf_op jit(solution)/shard_map/ppermute | solution.py:245
  59.6 1.9 %collective-permute-start.2 = (f32[64,512]{1,0:T(8,128)S(1)}, f32[64,512]{1,0:T(8,128)S(1)}, u32[]{:S(2)}, u32[]{:S(2)}) collective-permute-start(f32[64,512]{1,0:T(8,128)S(1)} %pad_maximum_fusion.1), channel_id=1, source_target_pairs={{0,8},{1,9},{2,10},{3,11},{4,12},{5,13},{6,14},{7,15},{8,0},{9,1},... | collective-permute-start | bytes 393224 | tf_op jit(solution)/shard_map/ppermute | solution.py:245
  61.6 7.5 %collective-permute-start.3 = (f32[64,512]{1,0:T(8,128)S(1)}, f32[64,512]{1,0:T(8,128)S(1)}, u32[]{:S(2)}, u32[]{:S(2)}) collective-permute-start(f32[64,512]{1,0:T(8,128)S(1)} %pad_maximum_fusion.1), channel_id=1, source_target_pairs={{0,12},{1,13},{2,14},{3,15},{4,8},{5,9},{6,10},{7,11},{8,4},{9,5},... | collective-permute-start | bytes 393224 | tf_op jit(solution)/shard_map/ppermute | solution.py:245
  69.1 4.8 %collective-permute-done.1 = f32[64,512]{1,0:T(8,128)S(1)} collective-permute-done((f32[64,512]{1,0:T(8,128)S(1)}, f32[64,512]{1,0:T(8,128)S(1)}, u32[]{:S(2)}, u32[]{:S(2)}) %collective-permute-start.1) | collective-permute-done | bytes 131104 | tf_op jit(solution)/shard_map/ppermute | solution.py:245
  74.0 2.0 %collective-permute-done.3 = f32[64,512]{1,0:T(8,128)S(1)} collective-permute-done((f32[64,512]{1,0:T(8,128)S(1)}, f32[64,512]{1,0:T(8,128)S(1)}, u32[]{:S(2)}, u32[]{:S(2)}) %collective-permute-start.3) | collective-permute-done | bytes 131104 | tf_op jit(solution)/shard_map/ppermute | solution.py:245
  76.0 3.3 %collective-permute-start.4 = (f32[256,512]{1,0:T(8,128)S(1)}, f32[256,512]{1,0:T(8,128)S(1)}, u32[]{:S(2)}, u32[]{:S(2)}) collective-permute-start(f32[256,512]{1,0:T(8,128)S(1)} %constant_dynamic-update-slice_fusion.own), channel_id=1, source_target_pairs={{0,1},{1,0},{2,3},{3,2},{4,5},{5,4},{6,7},{7,6},{8,9},{9,8},{10,11... | collective-permute-start | bytes 1572872 | tf_op jit(solution)/shard_map/ppermute | solution.py:278
  80.7 0.9 copy-done.4
  81.5 22.8 %child_cholesky.1 = (f32[32,512]{1,0:T(8,128)}, f32[128,512]{1,0:T(8,128)}, f32[128,512]{1,0:T(8,128)}) custom-call(s32[39]{0:T(128)} %compare_select_fusion.2.info, f32[256,512]{1,0:T(8,128)} %copy-done.3, f32[256,512]{1,0:T(8,128)} %copy-done.4, f32[128,512]{1,0:T(8,128)} %bitcast.14), custom_call_target="tpu_custom_call" | custom-call | tf_op jit(solution)/shard_map/child_cholesky/pallas_call | solution.py:280
  104.3 5.2 %update.1 = (f32[128,512]{1,0:T(8,128)}, f32[128,512]{1,0:T(8,128)}, f32[128,512]{1,0:T(8,128)}, f32[128,512]{1,0:T(8,128)}, f32[128,512]{1,0:T(8,128)}) custom-call(s32[39]{0:T(128)} %compare_select_fusion.2.info, f32[128,512]{1,0:T(8,128)} %get-tuple-element.23.w, f32[16,128,512]{2,1,0:T(8,128)} %all-gather.4.cloned.1.call-done.panels), custom_call_target="tpu_custom_call" | custom-call | tf_op jit(solution)/shard_map/update/pallas_call | solution.py:292
  109.6 1.9 %collective-permute-start.5 = (f32[128,512]{1,0:T(8,128)}, f32[128,512]{1,0:T(8,128)S(1)}, u32[]{:S(2)}, u32[]{:S(2)}) collective-permute-start(f32[128,512]{1,0:T(8,128)} %get-tuple-element.24), channel_id=1, source_target_pairs={{0,16},{16,0},{32,48},{48,32},{64,80},{80,64},{96,112},{112,96},{1... | collective-permute-start | bytes 786440 | tf_op jit(solution)/shard_map/ppermute | solution.py:306
  111.5 2.8 %collective-permute-start.6 = (f32[128,512]{1,0:T(8,128)}, f32[128,512]{1,0:T(8,128)S(1)}, u32[]{:S(2)}, u32[]{:S(2)}) collective-permute-start(f32[128,512]{1,0:T(8,128)} %get-tuple-element.25), channel_id=1, source_target_pairs={{0,32},{16,48},{32,0},{48,16},{64,96},{80,112},{96,64},{112,80},{1... | collective-permute-start | bytes 786440 | tf_op jit(solution)/shard_map/ppermute | solution.py:306
  114.3 4.9 %collective-permute-start.7 = (f32[128,512]{1,0:T(8,128)}, f32[128,512]{1,0:T(8,128)S(1)}, u32[]{:S(2)}, u32[]{:S(2)}) collective-permute-start(f32[128,512]{1,0:T(8,128)} %get-tuple-element.26), channel_id=1, source_target_pairs={{0,64},{16,80},{32,96},{48,112},{64,0},{80,16},{96,32},{112,48},{1... | collective-permute-start | bytes 786440 | tf_op jit(solution)/shard_map/ppermute | solution.py:306
  119.1 3.1 %collective-permute-start.8 = (f32[128,512]{1,0:T(8,128)}, f32[128,512]{1,0:T(8,128)S(1)}, u32[]{:S(2)}, u32[]{:S(2)}) collective-permute-start(f32[128,512]{1,0:T(8,128)} %get-tuple-element.27), channel_id=1, source_target_pairs={{0,128},{16,144},{32,160},{48,176},{64,192},{80,208},{96,224},{112... | collective-permute-start | bytes 786440 | tf_op jit(solution)/shard_map/ppermute | solution.py:306
  122.2 4.2 %collective-permute-start.9 = (f32[128,512]{1,0:T(8,128)}, f32[128,512]{1,0:T(8,128)S(1)}, u32[]{:S(2)}, u32[]{:S(2)}) collective-permute-start(f32[128,512]{1,0:T(8,128)} %get-tuple-element.28), channel_id=1, source_target_pairs={{0,256},{16,272},{32,288},{48,304},{64,320},{80,336},{96,352},{112... | collective-permute-start | bytes 786440 | tf_op jit(solution)/shard_map/ppermute | solution.py:306
  126.4 12.4 %collective-permute-done.6.r1 = f32[128,512]{1,0:T(8,128)S(1)} collective-permute-done((f32[128,512]{1,0:T(8,128)}, f32[128,512]{1,0:T(8,128)S(1)}, u32[]{:S(2)}, u32[]{:S(2)}) %collective-permute-start.6) | collective-permute-done | bytes 262176 | tf_op jit(solution)/shard_map/ppermute | solution.py:306
  139.9 4.0 %finish.1 = f32[512,512]{1,0:T(8,128)} custom-call(s32[39]{0:T(128)} %compare_select_fusion.2.info, f32[512,512]{1,0:T(8,128)} %bitcast.12, f32[128,512]{1,0:T(8,128)} %copy-done.5, f32[128,512]{1,0:T(8,128)} %copy-done.6, f32[128,512]{1,0:T(8,128)} %copy-done.7, f32[128,512]{1,0:T(8,128)} %copy-done.8, f32[128,512]{1,0:T(8,128)} %copy-done.9, ...), custom_call_target="tpu_custom_call" | custom-call | tf_op jit(solution)/shard_map/finish/pallas_call | solution.py:308
  (52 shorter events, 5.7 us)
Async XLA Ops:
  7.2 72.3 %copy-start.12 = (s32[32,16]{0,1:T(8,128)S(1)}, s32[32,16]{0,1:T(8,128)}, u32[]{:S(2)}) copy-start(s32[32,16]{0,1:T(8,128)} %param.9) | copy-start | bytes 6148
  7.2 72.3 %copy-start.11 = (s32[32,16]{0,1:T(8,128)S(1)}, s32[32,16]{0,1:T(8,128)}, u32[]{:S(2)}) copy-start(s32[32,16]{0,1:T(8,128)} %param.10) | copy-start | bytes 6148
  7.2 72.2 %copy-start.10 = (s32[32,16]{0,1:T(8,128)S(1)}, s32[32,16]{0,1:T(8,128)}, u32[]{:S(2)}) copy-start(s32[32,16]{0,1:T(8,128)} %param.11) | copy-start | bytes 6148
  7.2 97.2 %all-gather.4.cloned.1.call-start = ((), (), s32[]{:S(2)}) async-start(), calls=%async_computation | async-start | bytes 4456448 | tf_op jit(solution)/shard_map/all_gather | solution.py:247
  7.9 131.0 %all-gather.6.cloned.1.call-start = ((), (), s32[]{:S(2)}) async-start(), calls=%async_computation.1 | async-start | bytes 4456448 | tf_op jit(solution)/shard_map/all_gather | solution.py:272
  8.9 18.6 %copy-start = (f32[128,512]{1,0:T(8,128)}, f32[128,512]{1,0:T(8,128)S(1)}, u32[]{:S(2)}) copy-start(f32[128,512]{1,0:T(8,128)S(1)} %slice_bitcast_fusion.mine) | copy-start | bytes 786436
  9.0 8.6 %collective-permute-start.10 = (f32[128,512]{1,0:T(8,128)S(1)}, f32[128,512]{1,0:T(8,128)S(1)}, u32[]{:S(2)}, u32[]{:S(2)}) collective-permute-start(f32[128,512]{1,0:T(8,128)S(1)} %slice_bitcast_fusion.mine), channel_id=1, source_target_pairs={{0,2},{1,3},{2,0},{3,1},{16,18},{17,19},{18,16},{19,17},{32,34},{3... | collective-permute-start | bytes 786440 | tf_op jit(solution)/shard_map/ppermute | solution.py:253
  17.5 10.0 %copy-start.2 = (f32[128,512]{1,0:T(8,128)}, f32[128,512]{1,0:T(8,128)S(1)}, u32[]{:S(2)}) copy-start(f32[128,512]{1,0:T(8,128)S(1)} %collective-permute-done.10.near) | copy-start | bytes 786436
  17.6 10.0 %collective-permute-start.11 = (f32[256,512]{1,0:T(8,128)S(1)}, f32[256,512]{1,0:T(8,128)S(1)}, u32[]{:S(2)}, u32[]{:S(2)}) collective-permute-start(f32[256,512]{1,0:T(8,128)S(1)} %pad_maximum_fusion), channel_id=1, source_target_pairs={{0,1},{1,0},{2,3},{3,2},{16,17},{17,16},{18,19},{19,18},{32,33},{3... | collective-permute-start | bytes 1572872 | tf_op jit(solution)/shard_map/ppermute | solution.py:257
  49.6 7.2 %collective-permute-start = (f32[32,512]{1,0:T(8,128)}, f32[32,512]{1,0:T(8,128)S(1)}, u32[]{:S(2)}, u32[]{:S(2)}) collective-permute-start(f32[32,512]{1,0:T(8,128)} %bitcast.15), channel_id=1, source_target_pairs={{0,2},{1,3},{2,0},{3,1},{4,6},{5,7},{6,4},{7,5},{8,10},{9,11},{10,... | collective-permute-start | bytes 196616 | tf_op jit(solution)/shard_map/ppermute | solution.py:245
  57.7 16.3 %collective-permute-start.1 = (f32[64,512]{1,0:T(8,128)S(1)}, f32[64,512]{1,0:T(8,128)S(1)}, u32[]{:S(2)}, u32[]{:S(2)}) collective-permute-start(f32[64,512]{1,0:T(8,128)S(1)} %pad_maximum_fusion.1), channel_id=1, source_target_pairs={{0,4},{1,5},{2,6},{3,7},{4,0},{5,1},{6,2},{7,3},{8,12},{9,13},{10,... | collective-permute-start | bytes 393224 | tf_op jit(solution)/shard_map/ppermute | solution.py:245
  59.6 14.3 %collective-permute-start.2 = (f32[64,512]{1,0:T(8,128)S(1)}, f32[64,512]{1,0:T(8,128)S(1)}, u32[]{:S(2)}, u32[]{:S(2)}) collective-permute-start(f32[64,512]{1,0:T(8,128)S(1)} %pad_maximum_fusion.1), channel_id=1, source_target_pairs={{0,8},{1,9},{2,10},{3,11},{4,12},{5,13},{6,14},{7,15},{8,0},{9,1},... | collective-permute-start | bytes 393224 | tf_op jit(solution)/shard_map/ppermute | solution.py:245
  61.6 14.4 %collective-permute-start.3 = (f32[64,512]{1,0:T(8,128)S(1)}, f32[64,512]{1,0:T(8,128)S(1)}, u32[]{:S(2)}, u32[]{:S(2)}) collective-permute-start(f32[64,512]{1,0:T(8,128)S(1)} %pad_maximum_fusion.1), channel_id=1, source_target_pairs={{0,12},{1,13},{2,14},{3,15},{4,8},{5,9},{6,10},{7,11},{8,4},{9,5},... | collective-permute-start | bytes 393224 | tf_op jit(solution)/shard_map/ppermute | solution.py:245
  76.0 4.6 %copy-start.3 = (f32[256,512]{1,0:T(8,128)}, f32[256,512]{1,0:T(8,128)S(1)}, u32[]{:S(2)}) copy-start(f32[256,512]{1,0:T(8,128)S(1)} %constant_dynamic-update-slice_fusion.own) | copy-start | bytes 1572868
  76.0 4.6 %collective-permute-start.4 = (f32[256,512]{1,0:T(8,128)S(1)}, f32[256,512]{1,0:T(8,128)S(1)}, u32[]{:S(2)}, u32[]{:S(2)}) collective-permute-start(f32[256,512]{1,0:T(8,128)S(1)} %constant_dynamic-update-slice_fusion.own), channel_id=1, source_target_pairs={{0,1},{1,0},{2,3},{3,2},{4,5},{5,4},{6,7},{7,6},{8,9},{9,8},{10,11... | collective-permute-start | bytes 1572872 | tf_op jit(solution)/shard_map/ppermute | solution.py:278
  80.7 0.9 copy-start.4
  109.6 16.8 %collective-permute-start.5 = (f32[128,512]{1,0:T(8,128)}, f32[128,512]{1,0:T(8,128)S(1)}, u32[]{:S(2)}, u32[]{:S(2)}) collective-permute-start(f32[128,512]{1,0:T(8,128)} %get-tuple-element.24), channel_id=1, source_target_pairs={{0,16},{16,0},{32,48},{48,32},{64,80},{80,64},{96,112},{112,96},{1... | collective-permute-start | bytes 786440 | tf_op jit(solution)/shard_map/ppermute | solution.py:306
  111.5 27.4 %collective-permute-start.6 = (f32[128,512]{1,0:T(8,128)}, f32[128,512]{1,0:T(8,128)S(1)}, u32[]{:S(2)}, u32[]{:S(2)}) collective-permute-start(f32[128,512]{1,0:T(8,128)} %get-tuple-element.25), channel_id=1, source_target_pairs={{0,32},{16,48},{32,0},{48,16},{64,96},{80,112},{96,64},{112,80},{1... | collective-permute-start | bytes 786440 | tf_op jit(solution)/shard_map/ppermute | solution.py:306
  114.3 24.6 %collective-permute-start.7 = (f32[128,512]{1,0:T(8,128)}, f32[128,512]{1,0:T(8,128)S(1)}, u32[]{:S(2)}, u32[]{:S(2)}) collective-permute-start(f32[128,512]{1,0:T(8,128)} %get-tuple-element.26), channel_id=1, source_target_pairs={{0,64},{16,80},{32,96},{48,112},{64,0},{80,16},{96,32},{112,48},{1... | collective-permute-start | bytes 786440 | tf_op jit(solution)/shard_map/ppermute | solution.py:306
  119.1 19.7 %collective-permute-start.8 = (f32[128,512]{1,0:T(8,128)}, f32[128,512]{1,0:T(8,128)S(1)}, u32[]{:S(2)}, u32[]{:S(2)}) collective-permute-start(f32[128,512]{1,0:T(8,128)} %get-tuple-element.27), channel_id=1, source_target_pairs={{0,128},{16,144},{32,160},{48,176},{64,192},{80,208},{96,224},{112... | collective-permute-start | bytes 786440 | tf_op jit(solution)/shard_map/ppermute | solution.py:306
  122.2 16.6 %collective-permute-start.9 = (f32[128,512]{1,0:T(8,128)}, f32[128,512]{1,0:T(8,128)S(1)}, u32[]{:S(2)}, u32[]{:S(2)}) collective-permute-start(f32[128,512]{1,0:T(8,128)} %get-tuple-element.28), channel_id=1, source_target_pairs={{0,256},{16,272},{32,288},{48,304},{64,320},{80,336},{96,352},{112... | collective-permute-start | bytes 786440 | tf_op jit(solution)/shard_map/ppermute | solution.py:306
  126.4 12.5 %copy-start.5 = (f32[128,512]{1,0:T(8,128)}, f32[128,512]{1,0:T(8,128)S(1)}, u32[]{:S(2)}) copy-start(f32[128,512]{1,0:T(8,128)S(1)} %collective-permute-done.5.r0) | copy-start | bytes 786436
  138.8 0.9 copy-start.8
  138.9 1.0 copy-start.9
  (3 other events, 2.3 us)
Sparse Core Ops, SparseCore 0:
  10.1 51.8 all-gather.3
  64.2 48.0 all-gather.5
